TPU v7x, 32 devices: a whole 2x2x4 slice. The times are simulated.
32 devices in a mesh: row: 4 (over x, core), col: 8 (over z, y).
Axes of the slice: x: 2, y: 2, z: 4, core: 2. Of those that a mesh axis runs over, the one named last changes fastest.
Arguments:
- front: bfloat16 [24576, 24576], P('row', 'col'), may hold values from -6 to 6
- diag_inverse: bfloat16 [256, 256], replicated, as said below
- fill_pattern: int32 [384, 384], replicated, may hold values from 0 to 1, as said below
Outputs:
- updated: bfloat16 [24576, 24576], P('row', 'col')
Inputs may be any that keep to these rules, and one draw needn't show every extreme that they name: `fill_pattern`: symmetric, with ones on the diagonal. `diag_inverse`: lower triangular.
All inputs are finite; a program needn't handle non-finite values.
Results may differ from a plain program's by a relative error of at most 0.0045.
Values may be sent and summed in bfloat16 or wider, within the bound.
A program may use at most 128 MiB of HBM per device.

v0:
```python
import jax
import jax.numpy as jnp
from jax import lax
from jax.sharding import PartitionSpec as P

B = 64
P_SIZE = 256


def broadcast(block, axis, owner):
    block = jnp.where(lax.axis_index(axis) == owner, block, jnp.zeros_like(block))
    return lax.psum(block, axis)


def body(front, diag_inverse, fill_pattern):
    rows, cols = front.shape
    n_row = lax.axis_size("row")
    n_col = lax.axis_size("col")
    block = B
    width = P_SIZE
    panel_blocks = width // block
    row_id = lax.axis_index("row")
    col_id = lax.axis_index("col")
    owner = col_id < panel_blocks
    first = jnp.minimum(col_id, panel_blocks - 1)
    contract = (((1,), (1,)), ((), ()))
    total = jnp.zeros((rows, width), jnp.float32)
    for source_col in range(panel_blocks):
        piece = broadcast(front[:, :block], "col", source_col)
        weights_part = diag_inverse[:, source_col * block : (source_col + 1) * block]
        total = total + lax.dot_general(
            piece, weights_part, contract, preferred_element_type=jnp.float32
        )
    factor = total.astype(jnp.bfloat16)
    ratio = n_col // n_row
    local_rows = rows // block
    local_cols = cols // block
    grouped = factor.reshape(local_cols, ratio, block, width)
    chosen = lax.dynamic_index_in_dim(grouped, col_id // n_row, 1, keepdims=False).reshape(
        cols, width
    )
    col_factor = broadcast(chosen, "row", col_id % n_row)
    product = lax.dot_general(factor, col_factor, contract, preferred_element_type=jnp.float32)
    pattern_grid = fill_pattern.reshape(local_rows, n_row, local_cols, n_col)
    picked = lax.dynamic_index_in_dim(pattern_grid, row_id, 1, keepdims=False)
    picked = lax.dynamic_index_in_dim(picked, col_id, 2, keepdims=False)
    row_global = jnp.arange(local_rows, dtype=jnp.int32) * n_row + row_id
    col_global = jnp.arange(local_cols, dtype=jnp.int32) * n_col + col_id
    keep = picked.astype(jnp.float32)
    keep = keep * (row_global >= panel_blocks).astype(jnp.float32)[:, None]
    keep = keep * (col_global >= panel_blocks).astype(jnp.float32)[None, :]
    spread = jnp.repeat(keep, block, axis=1)
    updated = (
        front.astype(jnp.float32).reshape(local_rows, block, cols)
        - product.reshape(local_rows, block, cols) * spread[:, None, :]
    )
    updated = updated.reshape(rows, cols).astype(jnp.bfloat16)
    panel_piece = lax.dynamic_slice_in_dim(factor, first * block, block, 1)
    leading = jnp.where(owner, panel_piece, updated[:, :block])
    return updated.at[:, :block].set(leading)


def solution(mesh):
    return jax.shard_map(
        body,
        mesh=mesh,
        in_specs=(P("row", "col"), P(), P()),
        out_specs=P("row", "col"),
        check_vma=False,
    )
```

profile of v0, /device:TPU:25, one launch (start us, length us, event | category | flops | bytes accessed | tf_op | source)
XLA Modules:
  0.0 327.1 jit_solution(10627440459883034830)
XLA Ops:
  6.5 0.0 all-reduce.6.cloned.1.call-start
  6.5 4.2 %broadcast_select_fusion = (bf16[6144,64]{1,0:T(8,128)(2,1)}, bf16[6144,64]{1,0:T(8,128)(2,1)}, bf16[6144,64]{1,0:T(8,128)(2,1)}, bf16[6144,64]{1,0:T(8,128)(2,1)}) fusion(pred[]{:T(512)S(6)} %eq.20, bf16[6144,3072]{1,0:T(8,128)(2,1)} %param.5, pred[]{:T(512)S(6)} %eq.18, pred[]{:T(512)S(6)} %eq.19, pred[]{:T(512)S(6)} %eq.17), kind=kLoop, calls=%fused_computation.9 | loop fusion | flops 1572864 | bytes 3932164 | tf_op jit(solution)/shard_map/jit(_where)/select_n | solution.py:11
  10.8 0.0 all-reduce.6.cloned.1.call-update
  10.8 0.0 all-reduce.4.cloned.1.call-start
  10.9 211.3 %all-reduce.6.cloned.1.call-done = (bf16[6144,64]{1,0:T(8,128)(2,1)}, bf16[6144,64]{1,0:T(8,128)(2,1)}, bf16[6144,64]{1,0:T(8,128)(2,1)}, bf16[6144,64]{1,0:T(8,128)(2,1)}) async-done(((bf16[6144,64]{1,0:T(8,128)(2,1)}, bf16[6144,64]{1,0:T(8,128)(2,1)}, bf16[6144,64]{1,0:T(8,128)(2,1)}, bf16[6144,64]{1,0:T(8,128)(2,1)}), (bf16[6144,64]{1,0:T(8,128)(2,1)}, bf16[6144,64]{1,0:T(8,128)(2,1)}, ...) | async-done | bytes 3145744 | tf_op jit(solution)/shard_map/psum | solution.py:12
  222.1 2.5 fusion.6
  224.7 1.0 convolution_add_fusion.2
  225.7 0.3 copy-done
  226.1 1.0 convolution_add_fusion.1
  227.1 0.4 copy-done.2
  227.5 1.1 fusion.2
  228.6 1.3 dynamic-slice_select_fusion
  229.8 0.0 all-reduce.4.cloned.1.call-update
  229.9 7.3 %reshape.60 = s32[96,4,48,8]{3,2,1,0:T(8,128)} reshape(s32[384,384]{1,0:T(8,128)} %param.7) | data formatting | bytes 1179648 | tf_op jit(solution)/shard_map/reshape | solution.py:44
  237.2 3.8 %constant_dynamic-slice_fusion = s32[96,1,48,1]{3,2,1,0:T(8,128)} fusion(s32[96,4,48,8]{3,2,1,0:T(8,128)} %reshape.60, s32[]{:T(128)S(6)} %select_n.88, s32[]{:T(128)S(6)} %select_n.90), kind=kLoop, calls=%fused_computation.23 | loop fusion | bytes 36872 | tf_op jit(solution)/shard_map/jit(dynamic_index_in_dim)/dynamic_slice | solution.py:46
  241.0 2.6 copy.12
  243.5 0.1 fusion.8
  243.6 1.2 broadcast_in_dim.9
  244.8 2.9 copy.9
  247.7 0.7 compare_reduce_fusion
  248.5 24.3 %all-reduce.4.cloned.1.call-done = bf16[3072,256]{1,0:T(8,128)(2,1)} async-done(((bf16[3072,256]{1,0:T(8,128)(2,1)}), bf16[3072,256]{1,0:T(8,128)(2,1)}) %all-reduce.4.cloned.1.call-update) | async-done | bytes 1572880 | tf_op jit(solution)/shard_map/psum | solution.py:12
  272.8 27.9 %fusion.1 = bf16[6144,3072]{1,0:T(8,128)(2,1)} fusion(bf16[6144,3072]{1,0:T(8,128)(2,1)} %param.5, bf16[6144,256]{1,0:T(8,128)(2,1)S(1)} %fusion.2, bf16[3072,256]{1,0:T(8,128)(2,1)} %all-reduce.4.cloned.1.call-done, f32[96,3072]{1,0:T(8,128)} %copy.9), kind=kOutput, calls=%fused_computation.2 | convolution fusion | flops 9739173888 | bytes 81395712 | tf_op jit(solution)/shard_map/dot_general | solution.py:43
  300.7 4.0 %select_select_fusion = bf16[6144,64]{1,0:T(8,128)(2,1)} fusion(bf16[6144,3072]{1,0:T(8,128)(2,1)} %fusion.1, bf16[6144,256]{1,0:T(8,128)(2,1)S(1)} %fusion.2, s32[]{:T(128)S(6)} %select_n.92, pred[]{:T(512)S(6)} %lt.25, pred[]{:T(512)} %compare_reduce_fusion), kind=kLoop, calls=%fused_computation.7 | loop fusion | flops 786432 | bytes 2359302 | tf_op jit(solution)/shard_map/select.1
  304.8 15.5 %scatter.4 = bf16[6144,3072]{1,0:T(8,128)(2,1)} dynamic-update-slice(bf16[6144,3072]{1,0:T(8,128)(2,1)} %fusion.1, bf16[6144,64]{1,0:T(8,128)(2,1)} %select_select_fusion, s32[]{:T(128)} %constant.97.clone.1, s32[]{:T(128)} %constant.97.clone.1) | dynamic-update-slice | bytes 1572868 | tf_op jit(solution)/shard_map/scatter | solution.py:60
  (8 shorter events, 0.0 us)
Async XLA Ops:
  6.5 215.6 %all-reduce.6.cloned.1.call-start = ((), (), s32[]{:S(2)}) async-start(), calls=%async_computation.1 | async-start | bytes 12582912 | tf_op jit(solution)/shard_map/psum | solution.py:12
  10.8 211.4 %copy-start.3 = (bf16[256,256]{1,0:T(8,128)(2,1)S(1)}, bf16[256,256]{1,0:T(8,128)(2,1)}, u32[]{:S(2)}) copy-start(bf16[256,256]{1,0:T(8,128)(2,1)} %param.6) | copy-start | bytes 393220
  10.8 262.0 %all-reduce.4.cloned.1.call-start = ((), (), s32[]{:S(2)}) async-start(), calls=%async_computation | async-start | bytes 3145728 | tf_op jit(solution)/shard_map/psum | solution.py:12
  222.1 2.5 copy-start.1
  224.7 1.4 copy-start
  226.1 1.4 copy-start.2
Sparse Core Ops, SparseCore 0:
  11.7 210.3 all-reduce.5
  230.0 42.7 all-reduce.3
where the time goes:
time: 330 us; the launch traced here: 327 us
  waiting for transfers between devices  236 us (72%)
  local copies, waits for them, and re-layouts  34 us (10%)
  matrix products  33.5 us (10%)
  between operations  13.5 us (4%)
  other arithmetic  10.3 us (3%)
    psum x2, waiting for transfers between devices, broadcast(): return lax.psum(block, axis)  236 us
    dot_general x1, matrix products, body(): lax.dot_general(factor, col_factor, contract, preferred_element_type=jnp....  27.9 us
    scatter x1, local copies, waits for them, and re-layouts, body(): return updated.at[:, :block].set(leading)  15.5 us
    reshape x1, local copies, waits for them, and re-layouts, body(): pattern_grid = fill_pattern.reshape(local_rows, n_row, local_cols, n_col)  7.31 us
  transfers between devices with their start and end apart: 2, of which 2 were waited for; matrix products, arithmetic and copies ran while one was open for 6% of the time, Pallas kernels for 0%

commit v1 on v0

v1 whole, which is shorter than its diff:
```python
import functools

import jax
import jax.numpy as jnp
from jax import lax
from jax.experimental import pallas as pl
from jax.experimental.pallas import tpu as pltpu
from jax.sharding import PartitionSpec as P

B = 64
P_SIZE = 256
LANES = 128
AHEAD = 3
MESH = pl.DeviceIdType.MESH
NT = (((1,), (1,)), ((), ()))


def nt_dot(a, b):
    return lax.dot_general(a, b, NT, preferred_element_type=jnp.float32)


def nn_dot(a, b):
    return jnp.dot(a, b, preferred_element_type=jnp.float32)


def one_hot(shape, test):
    i = lax.broadcasted_iota(jnp.int32, shape, 0)
    j = lax.broadcasted_iota(jnp.int32, shape, 1)
    return jnp.where(test(i, j), 1.0, 0.0).astype(jnp.bfloat16)


def gather_kernel(
    n_row, n_col,
    front, diag, fill, out,
    source, pan, colp, fac, colf, keep, w_lo, w_hi,
    load_sem, source_sem, row_recv, row_send, col_recv, col_send,
):
    r = lax.axis_index("row")
    c = lax.axis_index("col")
    rows, cols = out.shape
    heads = P_SIZE // B
    ratio = n_col // n_row
    half = 2 * ratio * B
    step_rows = 2 * half
    step_cols = step_rows // ratio
    chunks = rows // step_rows
    outer, inner = 4, n_col // 4
    a = c // inner
    b = c % inner
    owner = c < heads
    x, core = r // 2, r % 2
    source_row = c % n_row
    source_x, source_core = source_row // 2, source_row % 2
    parity = c // n_row
    n_x = n_row // 2

    def load(k):
        part = pl.ds(pl.multiple_of(k * step_rows, step_rows), step_rows)
        return pltpu.make_async_copy(front.at[part], out.at[part], load_sem.at[k])

    def fetch():
        return pltpu.make_async_copy(front.at[:, 0:LANES], source, source_sem)

    def row_copy(k, h, slot, target):
        return pltpu.make_async_remote_copy(
            src_ref=pan.at[k, h], dst_ref=pan.at[k, h],
            send_sem=row_send.at[k, h, slot], recv_sem=row_recv.at[k, h],
            device_id=(r, target), device_id_type=MESH,
        )

    def row_sends(k, h, act):
        a_h, b_h = h // inner, h % inner

        @pl.when(b == b_h)
        def _():
            @pl.when(jnp.logical_and(a >= a_h, a < outer - 1))
            def _():
                act(row_copy(k, h, 0, c + inner))

            @pl.when(jnp.logical_and(a <= a_h, a > 0))
            def _():
                act(row_copy(k, h, 1, c - inner))

            for d in range(1, inner):
                act(row_copy(k, h, 1 + d, a * inner + (b + d) % inner))

    def col_copy(k, src, slot, target):
        return pltpu.make_async_remote_copy(
            src_ref=src, dst_ref=colp.at[k],
            send_sem=col_send.at[k, slot], recv_sem=col_recv.at[k],
            device_id=(target, c), device_id_type=MESH,
        )

    def col_local(k):
        return pltpu.make_async_copy(pan.at[k, :, :, parity], colp.at[k], col_recv.at[k])

    is_source = r == source_row
    is_relay = jnp.logical_and(core == source_core, x != source_x)

    def col_source_sends(k, act):
        @pl.when(is_source)
        def _():
            src = pan.at[k, :, :, parity]
            for d in range(1, n_x):
                act(col_copy(k, src, d, ((x + d) % n_x) * 2 + core))
            act(col_copy(k, src, 0, x * 2 + 1 - core))

    def col_relay_sends(k, act):
        @pl.when(is_relay)
        def _():
            act(col_copy(k, colp.at[k], 0, x * 2 + 1 - core))

    @pl.when(owner)
    def _():
        fetch().start()

    for k in range(chunks):
        load(k).start()

    barrier = pltpu.get_barrier_semaphore()

    @pl.when(a > 0)
    def _():
        pl.semaphore_signal(barrier, inc=1, device_id=(r, c - inner), device_id_type=MESH)

    @pl.when(a < outer - 1)
    def _():
        pl.semaphore_signal(barrier, inc=1, device_id=(r, c + inner), device_id_type=MESH)

    for d in range(1, inner):
        pl.semaphore_signal(
            barrier, inc=1, device_id=(r, a * inner + (b + d) % inner), device_id_type=MESH
        )
    for d in range(1, n_row):
        pl.semaphore_signal(barrier, inc=1, device_id=((r + d) % n_row, c), device_id_type=MESH)

    @pl.when(owner)
    def _():
        fetch().wait()
        to_lo = one_hot((LANES, LANES), lambda i, j: (i == j) & (i < B))
        to_hi = one_hot((LANES, LANES), lambda i, j: (i + B == j) & (i < B))

        def pack(k, _):
            at = pl.multiple_of(k * step_rows, step_rows)
            both = nn_dot(source[pl.ds(at, half), :], to_lo)
            both += nn_dot(source[pl.ds(at + half, half), :], to_hi)
            pan[k, c] = both.astype(jnp.bfloat16).reshape(2, ratio, B, LANES)
            return 0

        lax.fori_loop(0, chunks, pack, 0)

    extra = jnp.where(a > 0, 1, 0) + jnp.where(a < outer - 1, 1, 0)
    pl.semaphore_wait(barrier, inner - 1 + n_row - 1 + extra)

    def own_sends(k, act):
        for h in range(heads):
            @pl.when(c == h)
            def _():
                row_sends(k, h, act)

    for k in range(min(AHEAD, chunks)):
        own_sends(k, lambda copy: copy.start())

    def spread(shift):
        return one_hot(
            (P_SIZE, heads * LANES),
            lambda i, j: (i == (j // LANES) * B + j % LANES - shift)
            & (j % LANES >= shift) & (j % LANES < shift + B),
        )

    w_lo[...] = nn_dot(diag[...], spread(0)).astype(jnp.bfloat16)
    w_hi[...] = nn_dot(diag[...], spread(B)).astype(jnp.bfloat16)

    count = fill.shape[0]
    local_rows = rows // B
    pick = one_hot((local_rows, count), lambda i, j: j == i * n_row + r)
    picked = nn_dot(pick, fill[...].astype(jnp.float32).astype(jnp.bfloat16)).astype(jnp.bfloat16)

    def make_keep(j, _):
        at = pl.multiple_of(j * step_cols, step_cols)
        widen = one_hot(
            (count, step_cols), lambda i, l: i == ((at + l) // B) * n_col + c
        )
        wide = nn_dot(picked, widen)
        i = lax.broadcasted_iota(jnp.int32, wide.shape, 0)
        l = lax.broadcasted_iota(jnp.int32, wide.shape, 1)
        live = (i * n_row + r >= heads) & (((at + l) // B) * n_col + c >= heads)
        keep[:, pl.ds(at, step_cols)] = jnp.where(live, wide, 0.0)
        return 0

    lax.fori_loop(0, cols // step_cols, make_keep, 0)

    step_blocks = step_rows // B
    to_front = one_hot((P_SIZE, LANES), lambda i, l: (i == c * B + l) & (l < B))

    def tile(i, j):
        row_at = pl.multiple_of(i * step_rows, step_rows)
        col_at = pl.multiple_of(j * step_cols, step_cols)
        part = (pl.ds(row_at, step_rows), pl.ds(col_at, step_cols))
        product = nt_dot(fac[part[0], :], colf[part[1], :])
        marks = keep[pl.ds(pl.multiple_of(i * step_blocks, step_blocks), step_blocks), part[1]]
        masked = product.reshape(step_blocks, B, step_cols) * marks[:, None, :]
        value = out[part].astype(jnp.float32) - masked.reshape(step_rows, step_cols)
        out[part] = value.astype(jnp.bfloat16)

    def arrive(k):
        @pl.when(k + AHEAD < chunks)
        def _():
            own_sends(k + AHEAD, lambda copy: copy.start())

        for h in range(heads):
            @pl.when(c != h)
            def _():
                row_copy(k, h, 0, c).wait_recv()
                row_sends(k, h, lambda copy: copy.start())

        col_source_sends(k, lambda copy: copy.start())

        @pl.when(is_source)
        def _():
            col_local(k).start()

    def factors(k):
        packed = jnp.concatenate(
            [pan[k, h].reshape(half, LANES) for h in range(heads)], axis=1
        )
        at = pl.multiple_of(k * step_rows, step_rows)
        fac[pl.ds(at, half), :] = nt_dot(packed, w_lo[...]).astype(jnp.bfloat16)
        fac[pl.ds(at + half, half), :] = nt_dot(packed, w_hi[...]).astype(jnp.bfloat16)

    def col_factors(k):
        @pl.when(is_source)
        def _():
            col_local(k).wait()

        @pl.when(jnp.logical_not(is_source))
        def _():
            col_copy(k, colp.at[k], 0, r).wait_recv()

        col_relay_sends(k, lambda copy: copy.start())
        packed = jnp.concatenate(
            [colp[k, h].reshape(2 * B, LANES) for h in range(heads)], axis=1
        )
        at = pl.multiple_of(k * step_cols, step_cols)
        colf[pl.ds(at, 2 * B), :] = nt_dot(packed, w_lo[...]).astype(jnp.bfloat16)
        colf[pl.ds(at + 2 * B, 2 * B), :] = nt_dot(packed, w_hi[...]).astype(jnp.bfloat16)

    def wave(k):
        lax.fori_loop(0, k + 1, lambda j, _: (tile(k, j), 0)[1], 0)
        lax.fori_loop(0, k, lambda i, _: (tile(i, k), 0)[1], 0)

        @pl.when(owner)
        def _():
            at = pl.ds(pl.multiple_of(k * step_rows, step_rows), step_rows)
            piece = nn_dot(fac[at, :], to_front)
            old = out[at, 0:LANES].astype(jnp.float32)
            lane = lax.broadcasted_iota(jnp.int32, old.shape, 1)
            out[at, 0:LANES] = jnp.where(lane < B, piece, old).astype(jnp.bfloat16)

    def step(k, _):
        @pl.when(k < chunks)
        def _():
            arrive(k)
            factors(k)

        @pl.when(k > 0)
        def _():
            col_factors(k - 1)
            load(k - 1).wait()
            wave(k - 1)

        return 0

    lax.fori_loop(0, chunks + 1, step, 0)

    def drain(k, _):
        for h in range(heads):
            row_sends(k, h, lambda copy: copy.wait_send())
        col_source_sends(k, lambda copy: copy.wait_send())
        col_relay_sends(k, lambda copy: copy.wait_send())
        return 0

    lax.fori_loop(0, chunks, drain, 0)


def store_kernel(value, out, sems):
    parts = sems.shape[0]
    size = value.shape[0] // parts
    copies = [
        pltpu.make_async_copy(
            value.at[pl.ds(i * size, size)], out.at[pl.ds(i * size, size)], sems.at[i]
        )
        for i in range(parts)
    ]
    for copy in copies:
        copy.start()
    for copy in copies:
        copy.wait()


def body(front, diag_inverse, fill_pattern):
    rows, cols = front.shape
    n_row = lax.axis_size("row")
    n_col = lax.axis_size("col")
    heads = P_SIZE // B
    ratio = n_col // n_row
    step_rows = 4 * ratio * B
    chunks = rows // step_rows
    inner = n_col // 4
    bf16 = jnp.bfloat16
    any_space = pl.BlockSpec(memory_space=pl.ANY)
    vmem = pl.BlockSpec(memory_space=pltpu.VMEM)
    held = pl.pallas_call(
        functools.partial(gather_kernel, n_row, n_col),
        out_shape=pltpu.VMEM((rows, cols), bf16),
        in_specs=[any_space, vmem, vmem],
        out_specs=vmem,
        scratch_shapes=[
            pltpu.VMEM((rows, LANES), bf16),
            pltpu.VMEM((chunks, heads, 2, ratio, B, LANES), bf16),
            pltpu.VMEM((chunks, heads, 2, B, LANES), bf16),
            pltpu.VMEM((rows, P_SIZE), bf16),
            pltpu.VMEM((cols, P_SIZE), bf16),
            pltpu.VMEM((rows // B, cols), jnp.float32),
            pltpu.VMEM((P_SIZE, heads * LANES), bf16),
            pltpu.VMEM((P_SIZE, heads * LANES), bf16),
            pltpu.SemaphoreType.DMA((chunks,)),
            pltpu.SemaphoreType.DMA,
            pltpu.SemaphoreType.DMA((chunks, heads)),
            pltpu.SemaphoreType.DMA((chunks, heads, inner + 1)),
            pltpu.SemaphoreType.DMA((chunks,)),
            pltpu.SemaphoreType.DMA((chunks, n_row // 2)),
        ],
        compiler_params=pltpu.CompilerParams(
            collective_id=0, has_side_effects=True, vmem_limit_bytes=20 * 2**20
        ),
        name="gather_update",
    )(front, diag_inverse, fill_pattern)
    return pl.pallas_call(
        store_kernel,
        out_shape=jax.ShapeDtypeStruct((rows, cols), bf16),
        in_specs=[any_space],
        out_specs=any_space,
        scratch_shapes=[pltpu.SemaphoreType.DMA((chunks,))],
        compiler_params=pltpu.CompilerParams(vmem_limit_bytes=20 * 2**20),
        name="store",
    )(pltpu.with_memory_space_constraint(held, pltpu.VMEM))


def solution(mesh):
    return jax.shard_map(
        body,
        mesh=mesh,
        in_specs=(P("row", "col"), P(), P()),
        out_specs=P("row", "col"),
        check_vma=False,
    )
```

time: 330 us -> 253 us (0.77)
  Pallas kernels: 0 us -> 253 us
  waiting for transfers between devices: 236 us -> 0 us
  local copies, waits for them, and re-layouts: 34 us -> 0 us
  matrix products: 33.5 us -> 0 us
  between operations: 13.5 us -> 0.01 us
  other arithmetic: 10.3 us -> 0 us
    pallas_call x0 -> x2, Pallas kernels: none -> 253 us  [the longest x1 241 us: body(): pl.pallas_call(functools.partial(gather_kernel, n_row, n_col), out_shape=...]
    psum x2 -> x0, waiting for transfers between devices: 236 us -> none  [broadcast(): return lax.psum(block, axis)]
    dot_general x5 -> x0, matrix products: 33.5 us -> none  [the longest x1 27.9 us: body(): lax.dot_general(factor, col_factor, contract, preferred_element_type=jnp....]
    scatter x1 -> x0, local copies, waits for them, and re-layouts: 15.5 us -> none  [body(): return updated.at[:, :block].set(leading)]
    reshape x1 -> x0, local copies, waits for them, and re-layouts: 7.31 us -> none  [body(): pattern_grid = fill_pattern.reshape(local_rows, n_row, local_cols, n_col)]
    select_n x2 -> x0, other arithmetic: 5.49 us -> none  [broadcast(): jnp.where(lax.axis_index(axis) == owner, block, jnp.zeros_like(block))]
    another operation x2 -> x0, other arithmetic: 4.77 us -> none
    dynamic_slice x1 -> x0, local copies, waits for them, and re-layouts: 3.77 us -> none  [body(): picked = lax.dynamic_index_in_dim(picked, col_id, 2, keepdims=False)]
  transfers between devices with their start and end apart: 2 -> 0, of which waited for: 2 -> 0; matrix products, arithmetic and copies ran while one was open for 6% -> 0% of each run, Pallas kernels for 0% -> 0%
where the time goes in v1:
time: 253 us
  Pallas kernels  253 us (100%)
    pallas_call x1, Pallas kernels, body(): pl.pallas_call(functools.partial(gather_kernel, n_row, n_col), out_shape=...  241 us
    pallas_call x1, Pallas kernels, body(): pl.pallas_call(store_kernel, out_shape=jax.ShapeDtypeStruct((rows, cols),...  12.4 us

profile of v1, /device:TPU:25, one launch (start us, length us, event | category | flops | bytes accessed | tf_op | source)
XLA Modules:
  0.0 253.3 jit_solution(11318409910311003428)
XLA Ops:
  0.0 241.0 %gather_update.1.value = bf16[6144,3072]{1,0:T(8,128)(2,1)S(1)} custom-call(bf16[6144,3072]{1,0:T(8,128)(2,1)} %front.1, bf16[256,256]{1,0:T(8,128)(2,1)} %diag.1, s32[384,384]{1,0:T(8,128)} %fill.1), custom_call_target="tpu_custom_call" | custom-call | tf_op jit(solution)/shard_map/gather_update/pallas_call | solution.py:313
  241.0 12.4 %store.1 = bf16[6144,3072]{1,0:T(8,128)(2,1)} custom-call(bf16[6144,3072]{1,0:T(8,128)(2,1)S(1)} %gather_update.1.value), custom_call_target="tpu_custom_call" | custom-call | tf_op jit(solution)/shard_map/store/pallas_call | solution.py:339

commit v2 on v1

--- a/solution.py
+++ b/solution.py
@@ -10,7 +10,7 @@
 B = 64
 P_SIZE = 256
 LANES = 128
-AHEAD = 3
+AHEAD = 1
 MESH = pl.DeviceIdType.MESH
 NT = (((1,), (1,)), ((), ()))
 

time: 253 us -> 252 us (level)
  no operation moved by 1% of the time
where the time goes in v2:
time: 252 us
  Pallas kernels  252 us (100%)
    pallas_call x1, Pallas kernels, body(): pl.pallas_call(functools.partial(gather_kernel, n_row, n_col), out_shape=...  240 us
    pallas_call x1, Pallas kernels, body(): pl.pallas_call(store_kernel, out_shape=jax.ShapeDtypeStruct((rows, cols),...  12.4 us

profile of v2, /device:TPU:25, one launch (start us, length us, event | category | flops | bytes accessed | tf_op | source)
XLA Modules:
  0.0 252.2 jit_solution(15255157444472771241)
XLA Ops:
  0.0 239.8 %gather_update.1.value = bf16[6144,3072]{1,0:T(8,128)(2,1)S(1)} custom-call(bf16[6144,3072]{1,0:T(8,128)(2,1)} %front.1, bf16[256,256]{1,0:T(8,128)(2,1)} %diag.1, s32[384,384]{1,0:T(8,128)} %fill.1), custom_call_target="tpu_custom_call" | custom-call | tf_op jit(solution)/shard_map/gather_update/pallas_call | solution.py:313
  239.8 12.4 %store.1 = bf16[6144,3072]{1,0:T(8,128)(2,1)} custom-call(bf16[6144,3072]{1,0:T(8,128)(2,1)S(1)} %gather_update.1.value), custom_call_target="tpu_custom_call" | custom-call | tf_op jit(solution)/shard_map/store/pallas_call | solution.py:339
